TPU v7x, 256 devices: a whole 4x4x8 slice. The times are simulated.
256 devices in a mesh: row: 8 (over z), col: 32 (over y, x, core).
Axes of the slice: x: 4, y: 4, z: 8, core: 2. Of those that a mesh axis runs over, the one named last changes fastest.
Arguments:
- sources: float32 [30, 32768], P(None, ('row', 'col')), may hold values from -12 to 12
- log_source_mass: float32 [32768], P(('row', 'col')), may hold values from -4 to 4
- targets: float32 [30, 16384], P(None, 'col'), may hold values from -6 to 6
- log_target_mass: float32 [16384], P('col'), may hold values from -4 to 4
- start_potential: float32 [16384], P('col'), may hold values from -12 to 250
Outputs:
- row_potential: float32 [32768], P(('row', 'col'))
- column_potential: float32 [16384], P('col')
All inputs are finite; a program needn't handle non-finite values.
Results may differ from a plain program's by a relative error of at most 0.00015.
Values sent between devices are 32-bit elements; how exact they have to be, the bound alone decides.
No kernel may reach another device: no remote copies, remote signals or barrier semaphores. Data moves between devices by JAX's collectives and lax.ppermute only.
A program may use at most 64 MiB of HBM per device.

v0:
```python
import math
import jax
import jax.numpy as jnp
from jax import lax
from jax.sharding import PartitionSpec as P

ITERS = 2
entropic_scale = 2.0
lowest = -1e30
block_width = 2048


def merged(shard, axis, combine):
    everything = jax.tree.map(lambda part: lax.all_gather(part, axis), shard)
    leading = jax.tree.map(lambda part: part[0], everything)

    def lap(k, so_far):
        return combine(so_far, jax.tree.map(lambda part: part[k], everything))

    return lax.fori_loop(1, lax.axis_size(axis), lap, leading)


def tile_scores(own_coords, own_sq, other):
    dims = own_coords.shape[0]
    coords = other[:dims]
    inner = lax.dot_general(
        own_coords,
        coords,
        (((0,), (0,)), ((), ())),
        precision=lax.Precision.HIGHEST,
        preferred_element_type=jnp.float32,
    )
    other_sq = 0.5 * jnp.sum(coords * coords, axis=0)
    cost = own_sq[:, None] + other_sq[None, :] - inner
    return other[dims][None, :] - cost / entropic_scale


def merge_pair(first, second):
    peak = jnp.maximum(first[0], second[0])
    return (peak, first[1] * jnp.exp(first[0] - peak) + second[1] * jnp.exp(second[0] - peak))


def online_fold(own_coords, partial_value, piece):
    own_sq = 0.5 * jnp.sum(own_coords * own_coords, axis=0)
    length = piece.shape[1]
    width = math.gcd(length, block_width)
    blocks = piece.reshape(piece.shape[0], length // width, width).transpose(1, 0, 2)

    def advance(running, block):
        scores = tile_scores(own_coords, own_sq, block)
        block_max = jnp.max(scores, axis=1)
        block_sum = jnp.sum(jnp.exp(scores - block_max[:, None]), axis=1)
        return (merge_pair(running, (block_max, block_sum)), None)

    result, unused = lax.scan(advance, partial_value, blocks)
    return result


def column_partials(row_block, all_columns):
    dims = row_block.shape[0] - 1
    coords = all_columns[:dims]
    count = coords.shape[1]
    width = math.gcd(count, block_width)
    blocks = coords.reshape(dims, count // width, width).transpose(1, 0, 2)
    row_sq = 0.5 * jnp.sum(row_block[:dims] * row_block[:dims], axis=0)

    def one_block(block):
        inner = lax.dot_general(
            row_block[:dims],
            block,
            (((0,), (0,)), ((), ())),
            precision=lax.Precision.HIGHEST,
            preferred_element_type=jnp.float32,
        )
        cost = row_sq[:, None] + 0.5 * jnp.sum(block * block, axis=0)[None, :] - inner
        scores = row_block[dims][:, None] - cost / entropic_scale
        block_max = jnp.max(scores, axis=0)
        return (block_max, jnp.sum(jnp.exp(scores - block_max[None, :]), axis=0))

    peaks, totals = lax.map(one_block, blocks)
    return (peaks.reshape(count), totals.reshape(count))


def on_device(sources, log_source_mass, targets, log_target_mass, start_potential):
    own_rows = sources.shape[1]
    own_cols = targets.shape[1]
    target_term = start_potential / entropic_scale + log_target_mass
    row_potential = jnp.zeros((own_rows,), jnp.float32)
    column_potential = start_potential
    for sweep in range(ITERS):
        target_pack = jnp.concatenate([targets, target_term[None, :]], axis=0)
        row_start = (
            jnp.full((own_rows,), lowest, jnp.float32),
            jnp.zeros((own_rows,), jnp.float32),
        )
        gathered = lax.all_gather(target_pack, "col", axis=1, tiled=True)
        row_peak, row_total = online_fold(sources, row_start, gathered)
        row_potential = -entropic_scale * (row_peak + jnp.log(row_total))
        source_term = row_potential / entropic_scale + log_source_mass
        source_pack = jnp.concatenate([sources, source_term[None, :]], axis=0)
        wide_peak, wide_total = column_partials(source_pack, gathered)
        blocks_count = lax.axis_size("col")
        peak_rows, total_rows = (
            lax.all_to_all(
                wide_peak.reshape(blocks_count, own_cols),
                "col",
                split_axis=0,
                concat_axis=0,
                tiled=True,
            ),
            lax.all_to_all(
                wide_total.reshape(blocks_count, own_cols),
                "col",
                split_axis=0,
                concat_axis=0,
                tiled=True,
            ),
        )
        local_peak = jnp.max(peak_rows, axis=0)
        local_total = jnp.sum(total_rows * jnp.exp(peak_rows - local_peak[None, :]), axis=0)
        col_peak, col_total = merged((local_peak, local_total), "row", merge_pair)
        column_potential = -entropic_scale * (col_peak + jnp.log(col_total))
        target_term = column_potential / entropic_scale + log_target_mass
    return (row_potential, column_potential)


def solution(mesh):
    return jax.shard_map(
        on_device,
        mesh=mesh,
        in_specs=(P(None, ("row", "col")), P(("row", "col")), P(None, "col"), P("col"), P("col")),
        out_specs=(P(("row", "col")), P("col")),
        check_vma=False,
    )
```

profile of v0, /device:TPU:2, one launch (start us, length us, event | category | flops | bytes accessed | tf_op | source)
XLA Modules:
  0.0 385.1 jit_solution(970008191891067864)
XLA Ops:
  10.2 51.7 %all-gather.11.cloned.1.call-done = f32[31,16384]{1,0:T(8,128)} async-done(((f32[31,512]{1,0:T(8,128)}), f32[31,16384]{1,0:T(8,128)}) %all-gather.11.cloned.1.call-update) | async-done | bytes 2031632 | tf_op jit(solution)/shard_map/all_gather | solution.py:96
  61.8 2.8 copy.31
  66.1 42.5 %while.88 = (s32[]{:T(128)}, f32[128]{0:T(128)S(1)}, f32[128]{0:T(128)S(1)}, f32[8,31,2048]{2,0,1:T(8,128)}, f32[128]{0:T(128)S(1)}, /*index=5*/f32[30,128]{1,0:T(8,128)S(1)}, s32[]{:T(128)}, s32[]{:T(128)}, s32[]{}) while((s32[]{:T(128)}, f32[128]{0:T(128)S(1)}, f32[128]{0:T(128)S(1)}, f32[8,31,2048]{2,0,1:T(8,128)}, ...), condition=%wide.region_5.6_spmd.clone, body=%wide.region_1.5_spmd.clone.sunk | while | flops 96330496 | bytes 3158143 | solution.py:55
  68.9 2.3 fusion.49
  74.2 2.3 fusion.49
  84.8 2.3 fusion.49
  90.1 2.3 fusion.49
  95.4 2.3 fusion.49
  100.7 2.3 fusion.49
  106.0 2.3 fusion.49
  110.5 16.6 %while.84 = (s32[]{:T(128)}, f32[8,2048]{1,0:T(8,128)S(1)}, f32[8,2048]{1,0:T(8,128)S(1)}, f32[128]{0:T(128)S(1)}, f32[128]{0:T(128)S(1)}, /*index=5*/f32[8,30,2...) while((s32[]{:T(128)}, f32[8,2048]{1,0:T(8,128)S(1)}, f32[8,2048]{1,0:T(8,128)S(1)}, ...), condition=%wide.region_10.11_spmd, body=%wide.region_6.10_spmd.sunk | while | flops 96325632 | bytes 3186793 | solution.py:80
  127.8 5.8 %all-to-all-start = ((f32[32,1,512]{2,1,0:T(1,128)}), f32[32,1,512]{2,1,0:T(1,128)S(1)}, u32[]{:S(2)}, u32[]{:S(2)}) async-start(f32[32,1,512]{2,1,0:T(1,128)} %all_to_all.32), calls=%async_computation | async-start | bytes 131072 | tf_op jit(solution)/shard_map/all_to_all | solution.py:104
  134.4 5.6 %all-to-all-done = f32[32,1,512]{2,1,0:T(1,128)S(1)} async-done(((f32[32,1,512]{2,1,0:T(1,128)}), f32[32,1,512]{2,1,0:T(1,128)S(1)}, u32[]{:S(2)}, u32[]{:S(2)}) %all-to-all-start) | async-done | bytes 65568 | tf_op jit(solution)/shard_map/all_to_all | solution.py:104
  140.0 4.9 %all-to-all-start.1 = ((f32[32,1,512]{2,1,0:T(1,128)}), f32[32,1,512]{2,1,0:T(1,128)S(1)}, u32[]{:S(2)}, u32[]{:S(2)}) async-start(f32[32,1,512]{2,1,0:T(1,128)} %all_to_all.34), calls=%async_computation.1 | async-start | bytes 131072 | tf_op jit(solution)/shard_map/all_to_all | solution.py:111
  145.0 6.3 %all-to-all-done.1 = f32[32,1,512]{2,1,0:T(1,128)S(1)} async-done(((f32[32,1,512]{2,1,0:T(1,128)}), f32[32,1,512]{2,1,0:T(1,128)S(1)}, u32[]{:S(2)}, u32[]{:S(2)}) %all-to-all-start.1) | async-done | bytes 65568 | tf_op jit(solution)/shard_map/all_to_all | solution.py:111
  151.3 24.1 %all-gather.5 = f32[8,1,512]{2,1,0:T(1,128)S(1)} all-gather(f32[1,1,512]{2,1,0:T(1,128)S(1)} %bitcast.214), channel_id=3, replica_groups=mesh['row'=8,'col'=32] {'row'}, dimensions={0}, use_global_device_ids=true | all-gather | bytes 18432 | tf_op jit(solution)/shard_map/all_gather | solution.py:14
  175.4 21.5 %all-gather.4 = f32[8,1,512]{2,1,0:T(1,128)S(1)} all-gather(f32[1,1,512]{2,1,0:T(1,128)S(1)} %bitcast.213), channel_id=2, replica_groups=mesh['row'=8,'col'=32] {'row'}, dimensions={0}, use_global_device_ids=true | all-gather | bytes 18432 | tf_op jit(solution)/shard_map/all_gather | solution.py:14
  198.0 44.3 %all-gather.13.cloned.1.call-done = f32[31,16384]{1,0:T(8,128)} async-done(((f32[31,512]{1,0:T(8,128)}), f32[31,16384]{1,0:T(8,128)}) %all-gather.13.cloned.1.call-update) | async-done | bytes 2031632 | tf_op jit(solution)/shard_map/all_gather | solution.py:96
  242.3 2.8 copy.33
  246.6 42.5 %while.89 = (s32[]{:T(128)}, f32[128]{0:T(128)S(1)}, f32[128]{0:T(128)S(1)}, f32[8,31,2048]{2,0,1:T(8,128)}, f32[128]{0:T(128)S(1)}, /*index=5*/f32[30,128]{1,0:T(8,128)S(1)}, s32[]{:T(128)}, s32[]{:T(128)}, s32[]{}) while((s32[]{:T(128)}, f32[128]{0:T(128)S(1)}, f32[128]{0:T(128)S(1)}, f32[8,31,2048]{2,0,1:T(8,128)}, ...), condition=%wide.region_19.20_spmd.clone, body=%wide.region_15.0_spmd.clone.sunk | while | flops 96330496 | bytes 3158143 | solution.py:55
  249.4 2.3 fusion.52
  254.7 2.3 fusion.52
  260.0 2.3 fusion.52
  265.3 2.3 fusion.52
  270.6 2.3 fusion.52
  291.1 16.6 %while.86 = (s32[]{:T(128)}, f32[8,2048]{1,0:T(8,128)S(1)}, f32[8,2048]{1,0:T(8,128)S(1)}, f32[128]{0:T(128)S(1)}, f32[128]{0:T(128)S(1)}, /*index=5*/f32[8,30,2...) while((s32[]{:T(128)}, f32[8,2048]{1,0:T(8,128)S(1)}, f32[8,2048]{1,0:T(8,128)S(1)}, ...), condition=%wide.region_24.25_spmd, body=%wide.region_20.24_spmd.sunk | while | flops 96325632 | bytes 3186793 | solution.py:80
  308.4 5.8 %all-to-all-start.2 = ((f32[32,1,512]{2,1,0:T(1,128)}), f32[32,1,512]{2,1,0:T(1,128)S(1)}, u32[]{:S(2)}, u32[]{:S(2)}) async-start(f32[32,1,512]{2,1,0:T(1,128)} %all_to_all.38), calls=%async_computation.2 | async-start | bytes 131072 | tf_op jit(solution)/shard_map/all_to_all | solution.py:104
  314.9 5.6 %all-to-all-done.2 = f32[32,1,512]{2,1,0:T(1,128)S(1)} async-done(((f32[32,1,512]{2,1,0:T(1,128)}), f32[32,1,512]{2,1,0:T(1,128)S(1)}, u32[]{:S(2)}, u32[]{:S(2)}) %all-to-all-start.2) | async-done | bytes 65568 | tf_op jit(solution)/shard_map/all_to_all | solution.py:104
  320.5 4.9 %all-to-all-start.3 = ((f32[32,1,512]{2,1,0:T(1,128)}), f32[32,1,512]{2,1,0:T(1,128)S(1)}, u32[]{:S(2)}, u32[]{:S(2)}) async-start(f32[32,1,512]{2,1,0:T(1,128)} %all_to_all.40), calls=%async_computation.3 | async-start | bytes 131072 | tf_op jit(solution)/shard_map/all_to_all | solution.py:111
  325.5 6.3 %all-to-all-done.3 = f32[32,1,512]{2,1,0:T(1,128)S(1)} async-done(((f32[32,1,512]{2,1,0:T(1,128)}), f32[32,1,512]{2,1,0:T(1,128)S(1)}, u32[]{:S(2)}, u32[]{:S(2)}) %all-to-all-start.3) | async-done | bytes 65568 | tf_op jit(solution)/shard_map/all_to_all | solution.py:111
  331.8 24.1 %all-gather.7 = f32[8,1,512]{2,1,0:T(1,128)S(1)} all-gather(f32[1,1,512]{2,1,0:T(1,128)S(1)} %bitcast.215), channel_id=5, replica_groups=mesh['row'=8,'col'=32] {'row'}, dimensions={0}, use_global_device_ids=true | all-gather | bytes 18432 | tf_op jit(solution)/shard_map/all_gather | solution.py:14
  356.0 21.3 %all-gather.6 = f32[8,1,512]{2,1,0:T(1,128)S(1)} all-gather(f32[1,1,512]{2,1,0:T(1,128)S(1)} %bitcast.212), channel_id=4, replica_groups=mesh['row'=8,'col'=32] {'row'}, dimensions={0}, use_global_device_ids=true | all-gather | bytes 18432 | tf_op jit(solution)/shard_map/all_gather | solution.py:14
  (297 shorter events, 104.5 us)
Async XLA Ops:
  7.2 54.7 %all-gather.11.cloned.1.call-start = ((), (), s32[]{:S(2)}) async-start(), calls=%async_computation.4 | async-start | bytes 2162688 | tf_op jit(solution)/shard_map/all_gather | solution.py:96
  64.6 1.4 copy-start.3
  66.1 42.5 %copy-start = (f32[31,16384]{1,0:T(8,128)S(1)}, f32[31,16384]{1,0:T(8,128)}, u32[]{:S(2)}) copy-start(f32[31,16384]{1,0:T(8,128)} %all-gather.11.cloned.1.call-done) | copy-start | bytes 6094852
  109.8 0.7 copy-start.5
  110.5 86.8 %copy-start.4 = (f32[512]{0:T(512)S(1)}, f32[512]{0:T(512)}, u32[]{:S(2)}) copy-start(f32[512]{0:T(512)} %param.20) | copy-start | bytes 6148
  110.5 86.8 %copy-start.2 = (f32[30,512]{1,0:T(8,128)S(1)}, f32[30,512]{1,0:T(8,128)}, u32[]{:S(2)}) copy-start(f32[30,512]{1,0:T(8,128)} %param.19) | copy-start | bytes 184324
  127.8 12.1 %all-to-all-start = ((f32[32,1,512]{2,1,0:T(1,128)}), f32[32,1,512]{2,1,0:T(1,128)S(1)}, u32[]{:S(2)}, u32[]{:S(2)}) async-start(f32[32,1,512]{2,1,0:T(1,128)} %all_to_all.32), calls=%async_computation | async-start | bytes 131072 | tf_op jit(solution)/shard_map/all_to_all | solution.py:104
  140.0 11.3 %all-to-all-start.1 = ((f32[32,1,512]{2,1,0:T(1,128)}), f32[32,1,512]{2,1,0:T(1,128)S(1)}, u32[]{:S(2)}, u32[]{:S(2)}) async-start(f32[32,1,512]{2,1,0:T(1,128)} %all_to_all.34), calls=%async_computation.1 | async-start | bytes 131072 | tf_op jit(solution)/shard_map/all_to_all | solution.py:111
  144.9 97.5 %all-gather.13.cloned.1.call-start = ((), (), s32[]{:S(2)}) async-start(), calls=%async_computation.5 | async-start | bytes 2162688 | tf_op jit(solution)/shard_map/all_gather | solution.py:96
  246.6 42.5 %copy-start.1 = (f32[31,16384]{1,0:T(8,128)S(1)}, f32[31,16384]{1,0:T(8,128)}, u32[]{:S(2)}) copy-start(f32[31,16384]{1,0:T(8,128)} %all-gather.13.cloned.1.call-done) | copy-start | bytes 6094852
  308.4 12.1 %all-to-all-start.2 = ((f32[32,1,512]{2,1,0:T(1,128)}), f32[32,1,512]{2,1,0:T(1,128)S(1)}, u32[]{:S(2)}, u32[]{:S(2)}) async-start(f32[32,1,512]{2,1,0:T(1,128)} %all_to_all.38), calls=%async_computation.2 | async-start | bytes 131072 | tf_op jit(solution)/shard_map/all_to_all | solution.py:104
  320.5 11.3 %all-to-all-start.3 = ((f32[32,1,512]{2,1,0:T(1,128)}), f32[32,1,512]{2,1,0:T(1,128)S(1)}, u32[]{:S(2)}, u32[]{:S(2)}) async-start(f32[32,1,512]{2,1,0:T(1,128)} %all_to_all.40), calls=%async_computation.3 | async-start | bytes 131072 | tf_op jit(solution)/shard_map/all_to_all | solution.py:111
Sparse Core Ops, SparseCore 0:
  10.6 51.2 all-gather.10
  198.1 44.1 all-gather.12
where the time goes:
time: 387 us; the launch traced here: 385 us
  waiting for transfers between devices  120 us (31%)
  blocking collectives  91 us (24%)
  local copies, waits for them, and re-layouts  65.8 us (17%)
  matrix products  54.9 us (14%)
  starting transfers between devices  21.6 us (6%)
  other arithmetic  15.7 us (4%)
  between operations  14.3 us (4%)
    all_gather x2, waiting for transfers between devices, on_device(): gathered = lax.all_gather(target_pack, 'col', axis=1, tiled=True)  96 us
    all_gather x4, blocking collectives, merged(): everything = jax.tree.map(lambda part: lax.all_gather(part, axis), shard)  91 us
    dot_general x16, matrix products, tile_scores(): lax.dot_general(own_coords, coords, (((0,), (0,)), ((), ())), precision=l...  36.3 us
    slice x16, local copies, waits for them, and re-layouts, tile_scores(): coords = other[:dims]  28 us
    dot_general x16, matrix products, one_block(): lax.dot_general(row_block[:dims], block, (((0,), (0,)), ((), ())), precis...  18.6 us
    slice x16, local copies, waits for them, and re-layouts, tile_scores(): return other[dims][None, :] - cost / entropic_scale  13.7 us
    all_to_all x2, waiting for transfers between devices, on_device(): lax.all_to_all(wide_total.reshape(blocks_count, own_cols), 'col', split_a...  12.6 us
    all_to_all x2, starting transfers between devices, on_device(): lax.all_to_all(wide_peak.reshape(blocks_count, own_cols), 'col', split_ax...  11.7 us
  transfers between devices with their start and end apart: 6, of which 6 were waited for; matrix products, arithmetic and copies ran while one was open for 0% of the time, Pallas kernels for 0%

commit v1 on v0

--- a/solution.py
+++ b/solution.py
@@ -93,7 +93,9 @@
             jnp.full((own_rows,), lowest, jnp.float32),
             jnp.zeros((own_rows,), jnp.float32),
         )
-        gathered = lax.all_gather(target_pack, "col", axis=1, tiled=True)
+        gathered = jnp.concatenate(
+            lax.all_to_all(jnp.stack([target_pack] * lax.axis_size("col")), "col", 0, 0), axis=1
+        )
         row_peak, row_total = online_fold(sources, row_start, gathered)
         row_potential = -entropic_scale * (row_peak + jnp.log(row_total))
         source_term = row_potential / entropic_scale + log_source_mass

time: 387 us -> 355 us (0.917)
  waiting for transfers between devices: 120 us -> 79.9 us
  between operations: 14.3 us -> 0.88 us
  starting transfers between devices: 21.6 us -> 34.5 us
  local copies, waits for them, and re-layouts: 65.8 us -> 77.5 us
    all_gather x2 -> x0, waiting for transfers between devices: 96 us -> none  [on_device(): gathered = lax.all_gather(target_pack, 'col', axis=1, tiled=True)]
    all_to_all x0 -> x2, waiting for transfers between devices: none -> 55.9 us  [on_device(): lax.all_to_all(jnp.stack([target_pack] * lax.axis_size('col')), 'col', 0, 0)]
    all_to_all x0 -> x2, starting transfers between devices: none -> 12.9 us  [on_device(): lax.all_to_all(jnp.stack([target_pack] * lax.axis_size('col')), 'col', 0, 0)]
    another operation x4 -> x8, local copies, waits for them, and re-layouts: 0.02 us -> 9.59 us  [the longest x2 6.34 us: online_fold(): piece.reshape(piece.shape[0], length // width, width).transpose(1, 0, 2)]
    reshape x0 -> x4, local copies, waits for them, and re-layouts: none -> 9.24 us  [the longest x2 4.92 us: on_device(): jnp.concatenate(lax.all_to_all(jnp.stack([target_pack] * lax.axis_size('c...]
    unnamed x20 -> x12, local copies, waits for them, and re-layouts: 8.54 us -> 0.03 us
    slice x0 -> x2, local copies, waits for them, and re-layouts: none -> 4.85 us  [column_partials(): coords = all_columns[:dims]]
where the time goes in v1:
time: 355 us; the launch traced here: 353 us
  blocking collectives  89.7 us (25%)
  waiting for transfers between devices  79.9 us (23%)
  local copies, waits for them, and re-layouts  77.5 us (22%)
  matrix products  54.9 us (15%)
  starting transfers between devices  34.5 us (10%)
  other arithmetic  13.8 us (4%)
    all_gather x4, blocking collectives, merged(): everything = jax.tree.map(lambda part: lax.all_gather(part, axis), shard)  89.7 us
    all_to_all x2, waiting for transfers between devices, on_device(): lax.all_to_all(jnp.stack([target_pack] * lax.axis_size('col')), 'col', 0, 0)  55.9 us
    dot_general x16, matrix products, tile_scores(): lax.dot_general(own_coords, coords, (((0,), (0,)), ((), ())), precision=l...  36.3 us
    slice x16, local copies, waits for them, and re-layouts, tile_scores(): coords = other[:dims]  27.7 us
    dot_general x16, matrix products, one_block(): lax.dot_general(row_block[:dims], block, (((0,), (0,)), ((), ())), precis...  18.6 us
    slice x16, local copies, waits for them, and re-layouts, tile_scores(): return other[dims][None, :] - cost / entropic_scale  13.7 us
    all_to_all x2, starting transfers between devices, on_device(): lax.all_to_all(jnp.stack([target_pack] * lax.axis_size('col')), 'col', 0, 0)  12.9 us
    all_to_all x2, waiting for transfers between devices, on_device(): lax.all_to_all(wide_total.reshape(blocks_count, own_cols), 'col', split_a...  12.7 us
  transfers between devices with their start and end apart: 6, of which 6 were waited for; matrix products, arithmetic and copies ran while one was open for 0% of the time, Pallas kernels for 0%

profile of v1, /device:TPU:2, one launch (start us, length us, event | category | flops | bytes accessed | tf_op | source)
XLA Modules:
  0.0 353.0 jit_solution(15741075475678332288)
XLA Ops:
  3.8 7.8 %all-to-all-start = ((f32[32,31,512]{2,1,0:T(8,128)}), f32[32,31,512]{2,1,0:T(8,128)S(1)}, u32[]{:S(2)}, u32[]{:S(2)}) async-start(f32[32,31,512]{2,1,0:T(8,128)} %stack.4), calls=%async_computation | async-start | bytes 4194304 | tf_op jit(solution)/shard_map/all_to_all | solution.py:97
  11.6 27.9 %all-to-all-done = f32[32,31,512]{2,1,0:T(8,128)S(1)} async-done(((f32[32,31,512]{2,1,0:T(8,128)}), f32[32,31,512]{2,1,0:T(8,128)S(1)}, u32[]{:S(2)}, u32[]{:S(2)}) %all-to-all-start) | async-done | bytes 2031648 | tf_op jit(solution)/shard_map/all_to_all | solution.py:97
  39.5 2.5 copy.11
  41.9 3.2 reshape_reshape.4
  45.1 42.4 %while.88 = (s32[]{:T(128)}, f32[128]{0:T(128)S(1)}, f32[128]{0:T(128)S(1)}, f32[8,31,2048]{2,0,1:T(8,128)}, f32[128]{0:T(128)S(1)}, /*index=5*/f32[30,128]{1,0:T(8,128)S(1)}, s32[]{:T(128)}, s32[]{:T(128)}, s32[]{}) while((s32[]{:T(128)}, f32[128]{0:T(128)S(1)}, f32[128]{0:T(128)S(1)}, f32[8,31,2048]{2,0,1:T(8,128)}, ...), condition=%wide.region_5.6_spmd.clone, body=%wide.region_1.5_spmd.clone.sunk | while | flops 96330496 | bytes 3158143 | solution.py:55
  47.8 2.3 fusion.49
  58.4 2.3 fusion.49
  63.7 2.3 fusion.49
  74.3 2.3 fusion.49
  79.6 2.3 fusion.49
  84.9 2.3 fusion.49
  87.5 2.4 copy.13
  92.2 16.6 %while.84 = (s32[]{:T(128)}, f32[8,2048]{1,0:T(8,128)S(1)}, f32[8,2048]{1,0:T(8,128)S(1)}, f32[128]{0:T(128)S(1)}, f32[128]{0:T(128)S(1)}, /*index=5*/f32[8,30,2...) while((s32[]{:T(128)}, f32[8,2048]{1,0:T(8,128)S(1)}, f32[8,2048]{1,0:T(8,128)S(1)}, ...), condition=%wide.region_10.11_spmd, body=%wide.region_6.10_spmd.sunk | while | flops 96325632 | bytes 3186793 | solution.py:80
  109.5 5.9 %all-to-all-start.1 = ((f32[32,1,512]{2,1,0:T(1,128)}), f32[32,1,512]{2,1,0:T(1,128)S(1)}, u32[]{:S(2)}, u32[]{:S(2)}) async-start(f32[32,1,512]{2,1,0:T(1,128)} %all_to_all.39), calls=%async_computation.1 | async-start | bytes 131072 | tf_op jit(solution)/shard_map/all_to_all | solution.py:106
  116.1 5.7 %all-to-all-done.1 = f32[32,1,512]{2,1,0:T(1,128)S(1)} async-done(((f32[32,1,512]{2,1,0:T(1,128)}), f32[32,1,512]{2,1,0:T(1,128)S(1)}, u32[]{:S(2)}, u32[]{:S(2)}) %all-to-all-start.1) | async-done | bytes 65568 | tf_op jit(solution)/shard_map/all_to_all | solution.py:106
  121.7 4.9 %all-to-all-start.2 = ((f32[32,1,512]{2,1,0:T(1,128)}), f32[32,1,512]{2,1,0:T(1,128)S(1)}, u32[]{:S(2)}, u32[]{:S(2)}) async-start(f32[32,1,512]{2,1,0:T(1,128)} %all_to_all.41), calls=%async_computation.2 | async-start | bytes 131072 | tf_op jit(solution)/shard_map/all_to_all | solution.py:113
  126.7 6.3 %all-to-all-done.2 = f32[32,1,512]{2,1,0:T(1,128)S(1)} async-done(((f32[32,1,512]{2,1,0:T(1,128)}), f32[32,1,512]{2,1,0:T(1,128)S(1)}, u32[]{:S(2)}, u32[]{:S(2)}) %all-to-all-start.2) | async-done | bytes 65568 | tf_op jit(solution)/shard_map/all_to_all | solution.py:113
  133.1 25.6 %all-gather.5 = f32[8,1,512]{2,1,0:T(1,128)S(1)} all-gather(f32[1,1,512]{2,1,0:T(1,128)S(1)} %bitcast.200), channel_id=3, replica_groups=mesh['row'=8,'col'=32] {'row'}, dimensions={0}, use_global_device_ids=true | all-gather | bytes 18432 | tf_op jit(solution)/shard_map/all_gather | solution.py:14
  158.7 21.3 %all-gather.4 = f32[8,1,512]{2,1,0:T(1,128)S(1)} all-gather(f32[1,1,512]{2,1,0:T(1,128)S(1)} %bitcast.199), channel_id=2, replica_groups=mesh['row'=8,'col'=32] {'row'}, dimensions={0}, use_global_device_ids=true | all-gather | bytes 18432 | tf_op jit(solution)/shard_map/all_gather | solution.py:14
  182.0 5.1 %all-to-all-start.3 = ((f32[32,31,512]{2,1,0:T(8,128)}), f32[32,31,512]{2,1,0:T(8,128)S(1)}, u32[]{:S(2)}, u32[]{:S(2)}) async-start(f32[32,31,512]{2,1,0:T(8,128)} %stack.5), calls=%async_computation.3 | async-start | bytes 4194304 | tf_op jit(solution)/shard_map/all_to_all | solution.py:97
  187.2 28.0 %all-to-all-done.3 = f32[32,31,512]{2,1,0:T(8,128)S(1)} async-done(((f32[32,31,512]{2,1,0:T(8,128)}), f32[32,31,512]{2,1,0:T(8,128)S(1)}, u32[]{:S(2)}, u32[]{:S(2)}) %all-to-all-start.3) | async-done | bytes 2031648 | tf_op jit(solution)/shard_map/all_to_all | solution.py:97
  215.2 2.5 copy.15
  217.6 3.2 reshape_reshape.5
  220.8 42.4 %while.89 = (s32[]{:T(128)}, f32[128]{0:T(128)S(1)}, f32[128]{0:T(128)S(1)}, f32[8,31,2048]{2,0,1:T(8,128)}, f32[128]{0:T(128)S(1)}, /*index=5*/f32[30,128]{1,0:T(8,128)S(1)}, s32[]{:T(128)}, s32[]{:T(128)}, s32[]{}) while((s32[]{:T(128)}, f32[128]{0:T(128)S(1)}, f32[128]{0:T(128)S(1)}, f32[8,31,2048]{2,0,1:T(8,128)}, ...), condition=%wide.region_19.20_spmd.clone, body=%wide.region_15.0_spmd.clone.sunk | while | flops 96330496 | bytes 3158143 | solution.py:55
  263.2 2.4 copy.17
  268.3 16.6 %while.86 = (s32[]{:T(128)}, f32[8,2048]{1,0:T(8,128)S(1)}, f32[8,2048]{1,0:T(8,128)S(1)}, f32[128]{0:T(128)S(1)}, f32[128]{0:T(128)S(1)}, /*index=5*/f32[8,30,2...) while((s32[]{:T(128)}, f32[8,2048]{1,0:T(8,128)S(1)}, f32[8,2048]{1,0:T(8,128)S(1)}, ...), condition=%wide.region_24.25_spmd, body=%wide.region_20.24_spmd.sunk | while | flops 96325632 | bytes 3186793 | solution.py:80
  285.6 5.9 %all-to-all-start.4 = ((f32[32,1,512]{2,1,0:T(1,128)}), f32[32,1,512]{2,1,0:T(1,128)S(1)}, u32[]{:S(2)}, u32[]{:S(2)}) async-start(f32[32,1,512]{2,1,0:T(1,128)} %all_to_all.46), calls=%async_computation.4 | async-start | bytes 131072 | tf_op jit(solution)/shard_map/all_to_all | solution.py:106
  292.2 5.7 %all-to-all-done.4 = f32[32,1,512]{2,1,0:T(1,128)S(1)} async-done(((f32[32,1,512]{2,1,0:T(1,128)}), f32[32,1,512]{2,1,0:T(1,128)S(1)}, u32[]{:S(2)}, u32[]{:S(2)}) %all-to-all-start.4) | async-done | bytes 65568 | tf_op jit(solution)/shard_map/all_to_all | solution.py:106
  297.9 4.9 %all-to-all-start.5 = ((f32[32,1,512]{2,1,0:T(1,128)}), f32[32,1,512]{2,1,0:T(1,128)S(1)}, u32[]{:S(2)}, u32[]{:S(2)}) async-start(f32[32,1,512]{2,1,0:T(1,128)} %all_to_all.48), calls=%async_computation.5 | async-start | bytes 131072 | tf_op jit(solution)/shard_map/all_to_all | solution.py:113
  302.9 6.3 %all-to-all-done.5 = f32[32,1,512]{2,1,0:T(1,128)S(1)} async-done(((f32[32,1,512]{2,1,0:T(1,128)}), f32[32,1,512]{2,1,0:T(1,128)S(1)}, u32[]{:S(2)}, u32[]{:S(2)}) %all-to-all-start.5) | async-done | bytes 65568 | tf_op jit(solution)/shard_map/all_to_all | solution.py:113
  309.3 21.4 %all-gather.7 = f32[8,1,512]{2,1,0:T(1,128)S(1)} all-gather(f32[1,1,512]{2,1,0:T(1,128)S(1)} %bitcast.201), channel_id=5, replica_groups=mesh['row'=8,'col'=32] {'row'}, dimensions={0}, use_global_device_ids=true | all-gather | bytes 18432 | tf_op jit(solution)/shard_map/all_gather | solution.py:14
  330.7 21.4 %all-gather.6 = f32[8,1,512]{2,1,0:T(1,128)S(1)} all-gather(f32[1,1,512]{2,1,0:T(1,128)S(1)} %bitcast.198), channel_id=4, replica_groups=mesh['row'=8,'col'=32] {'row'}, dimensions={0}, use_global_device_ids=true | all-gather | bytes 18432 | tf_op jit(solution)/shard_map/all_gather | solution.py:14
  (293 shorter events, 117.2 us)
Async XLA Ops:
  3.8 7.8 %copy-start.1 = (f32[30,128]{1,0:T(8,128)S(1)}, f32[30,128]{1,0:T(8,128)}, u32[]{:S(2)}) copy-start(f32[30,128]{1,0:T(8,128)} %param.17) | copy-start | bytes 46084
  3.8 35.7 %all-to-all-start = ((f32[32,31,512]{2,1,0:T(8,128)}), f32[32,31,512]{2,1,0:T(8,128)S(1)}, u32[]{:S(2)}, u32[]{:S(2)}) async-start(f32[32,31,512]{2,1,0:T(8,128)} %stack.4), calls=%async_computation | async-start | bytes 4194304 | tf_op jit(solution)/shard_map/all_to_all | solution.py:97
  89.9 2.2 copy-start.3
  92.2 88.2 %copy-start.2 = (f32[512]{0:T(512)S(1)}, f32[512]{0:T(512)}, u32[]{:S(2)}) copy-start(f32[512]{0:T(512)} %param.20) | copy-start | bytes 6148
  92.2 88.2 %copy-start = (f32[30,512]{1,0:T(8,128)S(1)}, f32[30,512]{1,0:T(8,128)}, u32[]{:S(2)}) copy-start(f32[30,512]{1,0:T(8,128)} %param.19) | copy-start | bytes 184324
  109.5 12.3 %all-to-all-start.1 = ((f32[32,1,512]{2,1,0:T(1,128)}), f32[32,1,512]{2,1,0:T(1,128)S(1)}, u32[]{:S(2)}, u32[]{:S(2)}) async-start(f32[32,1,512]{2,1,0:T(1,128)} %all_to_all.39), calls=%async_computation.1 | async-start | bytes 131072 | tf_op jit(solution)/shard_map/all_to_all | solution.py:106
  121.7 11.3 %all-to-all-start.2 = ((f32[32,1,512]{2,1,0:T(1,128)}), f32[32,1,512]{2,1,0:T(1,128)S(1)}, u32[]{:S(2)}, u32[]{:S(2)}) async-start(f32[32,1,512]{2,1,0:T(1,128)} %all_to_all.41), calls=%async_computation.2 | async-start | bytes 131072 | tf_op jit(solution)/shard_map/all_to_all | solution.py:113
  182.0 33.1 %all-to-all-start.3 = ((f32[32,31,512]{2,1,0:T(8,128)}), f32[32,31,512]{2,1,0:T(8,128)S(1)}, u32[]{:S(2)}, u32[]{:S(2)}) async-start(f32[32,31,512]{2,1,0:T(8,128)} %stack.5), calls=%async_computation.3 | async-start | bytes 4194304 | tf_op jit(solution)/shard_map/all_to_all | solution.py:97
  285.6 12.3 %all-to-all-start.4 = ((f32[32,1,512]{2,1,0:T(1,128)}), f32[32,1,512]{2,1,0:T(1,128)S(1)}, u32[]{:S(2)}, u32[]{:S(2)}) async-start(f32[32,1,512]{2,1,0:T(1,128)} %all_to_all.46), calls=%async_computation.4 | async-start | bytes 131072 | tf_op jit(solution)/shard_map/all_to_all | solution.py:106
  297.9 11.3 %all-to-all-start.5 = ((f32[32,1,512]{2,1,0:T(1,128)}), f32[32,1,512]{2,1,0:T(1,128)S(1)}, u32[]{:S(2)}, u32[]{:S(2)}) async-start(f32[32,1,512]{2,1,0:T(1,128)} %all_to_all.48), calls=%async_computation.5 | async-start | bytes 131072 | tf_op jit(solution)/shard_map/all_to_all | solution.py:113
